TPU v7x, 256 devices: a whole 4x4x8 slice. The times are simulated.
256 devices in a mesh: row: 16 (over x_lo, y, core), col: 16 (over z, x_hi).
Axes of the slice: x: 4 (x_hi: 2, x_lo: 2; x = x_hi * 2 + x_lo), y: 4, z: 8, core: 2. Of those that a mesh axis runs over, the one named last changes fastest.
Arguments:
- block_vecs: float32 [16, 131072], P(None, ('col', 'row')), may hold values from -130 to 130
- direction: float32 [16, 131072], P(None, ('col', 'row')), may hold values from -130 to 130
- blocks: bfloat16 [1024, 32, 128, 128], P('col', 'row'), may hold values from 0 to 4
- block_cols: int32 [1024, 32], P('col', 'row'), may hold values from 0 to 1023, as said below
- live_counts: int32 [1024, 16], P('col', 'row'), may hold values from 1 to 2, as said below
Outputs:
- x_next: float32 [16, 131072], P(None, ('col', 'row'))
- reduced: float32 [48, 48], replicated
- residual: float32 [16, 131072], P(None, ('col', 'row'))
Inputs may be any that keep to these rules, and one draw needn't show every extreme that they name: `block_cols`: A block column index g in slots 2 * r to 2 * r + 1 of any block row satisfies (g // 4) mod 16 == r. `live_counts`: every block row has 2 live slots in at least one segment.
All inputs are finite; a program needn't handle non-finite values.
Results may differ from a plain program's by a relative error of at most 0.0003.
Values sent between devices are 32-bit elements; how exact they have to be, the bound alone decides.
A program may use at most 64 MiB of HBM per device.

v0:
```python
import math
import jax
import jax.numpy as jnp
from jax import lax
from jax.sharding import PartitionSpec as P

highest = lax.Precision.HIGHEST


def outer(left, right):
    return jnp.dot(left, right.T, precision=highest, preferred_element_type=jnp.float32)


def cholesky_lower(matrix):
    order_small = matrix.shape[0]
    places = jnp.arange(order_small, dtype=jnp.int32)

    def column_step(step, lower):
        pick = (places == step).astype(jnp.float32)
        row_now = jnp.sum(lower * pick[:, None], axis=0)
        column_now = jnp.sum(matrix * pick[None, :], axis=1)
        pivot = jnp.sum(column_now * pick) - jnp.sum(row_now * row_now)
        pivot_root = jnp.sqrt(pivot)
        below = (column_now - jnp.sum(lower * row_now[None, :], axis=1)) / pivot_root
        values = jnp.where(places > step, below, jnp.where(places == step, pivot_root, 0.0))
        return lower + values[:, None] * pick[None, :]

    return lax.fori_loop(0, order_small, column_step, jnp.zeros_like(matrix))


def solve_lower(lower, right):
    order_small = lower.shape[0]
    places = jnp.arange(order_small, dtype=jnp.int32)

    def row_step(step, solved):
        pick = (places == step).astype(jnp.float32)
        row_now = jnp.sum(lower * pick[:, None], axis=0)
        pivot = jnp.sum(row_now * pick)
        right_row = jnp.sum(right * pick[:, None], axis=0)
        value = (right_row - jnp.sum(row_now[:, None] * solved, axis=0)) / pivot
        return solved + pick[:, None] * value[None, :]

    return lax.fori_loop(0, order_small, row_step, jnp.zeros_like(right))


def solve_upper_t(lower, right):
    order_small = lower.shape[0]
    places = jnp.arange(order_small, dtype=jnp.int32)

    def row_step(count, solved):
        step = order_small - 1 - count
        pick = (places == step).astype(jnp.float32)
        column_now = jnp.sum(lower * pick[None, :], axis=1)
        pivot = jnp.sum(column_now * pick)
        right_row = jnp.sum(right * pick[:, None], axis=0)
        value = (right_row - jnp.sum(column_now[:, None] * solved, axis=0)) / pivot
        return solved + pick[:, None] * value[None, :]

    return lax.fori_loop(0, order_small, row_step, jnp.zeros_like(right))


def local_layout(block_cols, live_counts, span_rows, block_size, row_count):
    per_span = span_rows // block_size
    span_index = block_cols // per_span
    local_cols = span_index // row_count * per_span + block_cols % per_span
    slot_count = block_cols.shape[1]
    live_mask = (jnp.arange(slot_count, dtype=jnp.int32)[None, :] < live_counts).astype(jnp.float32)
    return (local_cols, live_mask)


def forward_part(col_panel, blocks, local_cols, live_mask):
    vec_width = col_panel.shape[0]
    block_size = blocks.shape[2]
    col_blocks = col_panel.reshape(vec_width, -1, block_size)
    picked = col_blocks[:, local_cols, :] * live_mask[None, :, :, None]
    forward = jnp.einsum(
        "vbkj,bkij->vbi", picked, blocks, precision=highest, preferred_element_type=jnp.float32
    )
    return 0.5 * forward.reshape(vec_width, -1)


def backward_part(row_panel, col_length, blocks, local_cols, live_mask):
    vec_width = row_panel.shape[0]
    block_size = blocks.shape[2]
    row_blocks = row_panel.reshape(vec_width, -1, block_size)
    backward = (
        jnp.einsum(
            "vbi,bkij->vbkj",
            row_blocks,
            blocks,
            precision=highest,
            preferred_element_type=jnp.float32,
        )
        * live_mask[None, :, :, None]
    )
    spread = jnp.zeros((vec_width, col_length // block_size, block_size), jnp.float32)
    spread = spread.at[:, local_cols.reshape(-1), :].add(
        backward.reshape(vec_width, -1, block_size)
    )
    return 0.5 * spread.reshape(vec_width, -1)


def per_device(block_vecs, direction, blocks, block_cols, live_counts):
    row_count = lax.axis_size("row")
    col_count = lax.axis_size("col")
    vec_width = block_vecs.shape[0]
    span_rows = block_vecs.shape[1]
    order_total = span_rows * row_count * col_count
    col_length = span_rows * col_count
    block_size = blocks.shape[2]
    local_cols, live_mask = local_layout(block_cols, live_counts, span_rows, block_size, row_count)
    paired = jnp.concatenate([block_vecs, direction], axis=0)
    pair_cols = lax.all_gather(paired, "col", axis=1, tiled=True)
    pair_rows = lax.all_gather(paired, "row", axis=1, tiled=True)
    forward = forward_part(pair_cols, blocks, local_cols, live_mask)
    backward = backward_part(pair_rows, col_length, blocks, local_cols, live_mask)
    image_pair = lax.psum_scatter(
        forward, "row", scatter_dimension=1, tiled=True
    ) + lax.psum_scatter(backward, "col", scatter_dimension=1, tiled=True)
    image_x = image_pair[:vec_width]
    image_p = image_pair[vec_width:]
    gram_x, cross_x = lax.psum(
        (outer(block_vecs, block_vecs), outer(block_vecs, image_x)), ("row", "col")
    )
    factor_x = cholesky_lower(gram_x)
    coefficient = solve_upper_t(factor_x, solve_lower(factor_x, cross_x))
    resid = image_x - jnp.dot(
        coefficient.T, block_vecs, precision=highest, preferred_element_type=jnp.float32
    )
    basis = jnp.concatenate([block_vecs, resid, direction], axis=0)
    resid_cols = lax.all_gather(resid, "col", axis=1, tiled=True)
    resid_rows = lax.all_gather(resid, "row", axis=1, tiled=True)
    forward_r = forward_part(resid_cols, blocks, local_cols, live_mask)
    column_x = outer(basis, image_x)
    column_p = outer(basis, image_p)
    backward_r = backward_part(resid_rows, col_length, blocks, local_cols, live_mask)
    image_r = lax.psum_scatter(
        forward_r, "row", scatter_dimension=1, tiled=True
    ) + lax.psum_scatter(backward_r, "col", scatter_dimension=1, tiled=True)
    column_r = outer(basis, image_r)
    gram_apply = jnp.concatenate([column_x, column_r, column_p], axis=1)
    gram_basis, gram_apply = lax.psum((outer(basis, basis), gram_apply), ("row", "col"))
    factor = cholesky_lower(gram_basis)
    halfway = solve_lower(factor, 0.5 * (gram_apply + gram_apply.T))
    reduced = solve_lower(factor, halfway.T)
    shifted = reduced + 3.0 * jnp.eye(3 * vec_width, dtype=jnp.float32)
    target = jnp.dot(
        shifted, shifted[:, :vec_width], precision=highest, preferred_element_type=jnp.float32
    )
    mixing = solve_upper_t(factor, target)
    fresh = jnp.dot(mixing.T, basis, precision=highest, preferred_element_type=jnp.float32)
    gram_fresh = lax.psum(outer(fresh, fresh), ("row", "col"))
    factor_fresh = cholesky_lower(gram_fresh)
    x_next = math.sqrt(order_total) * solve_lower(factor_fresh, fresh)
    return (x_next, reduced, resid)


def solution(mesh):
    return jax.shard_map(
        per_device,
        mesh=mesh,
        in_specs=(
            P(None, ("col", "row")),
            P(None, ("col", "row")),
            P("col", "row", None, None),
            P("col", "row"),
            P("col", "row"),
        ),
        out_specs=(P(None, ("col", "row")), P(), P(None, ("col", "row"))),
        check_vma=False,
    )
```

profile of v0, /device:TPU:1, one launch (start us, length us, event | category | flops | bytes accessed | tf_op | source)
XLA Modules:
  0.0 1421.3 jit_solution(11187509048310806808)
XLA Ops:
  11.9 37.2 %all-gather.5.cloned.1.call-done = f32[32,8192]{1,0:T(8,128)} async-done(((f32[32,512]{1,0:T(8,128)}), f32[32,8192]{1,0:T(8,128)}) %all-gather.5.cloned.1.call-update) | async-done | bytes 1048592 | tf_op jit(solution)/shard_map/all_gather | solution.py:114
  49.0 1.4 copy.57
  50.4 4.3 convolution_multiply_fusion
  54.9 5.7 scatter_fusion
  60.6 1.1 copy_bitcast_fusion
  62.0 64.4 %all-gather.3.cloned.1.call-done = f32[32,8192]{1,0:T(8,128)} async-done(((f32[32,512]{1,0:T(8,128)}), f32[32,8192]{1,0:T(8,128)}) %all-gather.3.cloned.1.call-update) | async-done | bytes 1048592 | tf_op jit(solution)/shard_map/all_gather | solution.py:113
  126.4 1.4 copy_bitcast_fusion.2
  128.6 6.0 fusion.45
  134.6 1.1 copy.69
  135.9 192.4 %reduce-scatter.7.cloned.1.call-done = f32[32,512]{1,0:T(8,128)} async-done(((f32[32,8192]{1,0:T(8,128)}), f32[32,512]{1,0:T(8,128)}) %reduce-scatter.7.cloned.1.call-update) | async-done | bytes 65552 | tf_op jit(solution)/shard_map/reduce_scatter | solution.py:119
  328.3 66.4 %reduce-scatter.5.cloned.1.call-done = f32[32,512]{1,0:T(8,128)} async-done(((f32[32,8192]{1,0:T(8,128)}), f32[32,512]{1,0:T(8,128)}) %reduce-scatter.5.cloned.1.call-update) | async-done | bytes 65552 | tf_op jit(solution)/shard_map/reduce_scatter | solution.py:117
  394.7 0.9 add.271
  395.7 78.8 %all-reduce.1 = (f32[16,16]{0,1:T(8,128)S(1)}, f32[16,16]{1,0:T(8,128)S(1)}) all-reduce(f32[16,16]{0,1:T(8,128)S(1)} %convolution_bitcast_fusion.1, f32[16,16]{1,0:T(8,128)S(1)} %fusion.72), channel_id=1, replica_groups=mesh['row'=16,'col'=16] {'row','col'}, use_global_device_ids=true, to_apply=%region_11.12 | all-reduce | flops 512 | bytes 4096 | tf_op jit(solution)/shard_map/psum | solution.py:122
  474.5 37.0 %while.135 = (s32[]{:T(128)}, f32[16,16]{1,0:T(8,128)S(1)}, f32[16,16]{1,0:T(8,128)S(1)}, s32[]{:T(128)}, s32[]{:T(128)}) while((s32[]{:T(128)}, f32[16,16]{1,0:T(8,128)S(1)}, f32[16,16]{1,0:T(8,128)S(1)}, s32[]{:T(128)}, s32[]{:T(128)}) %tuple.302), condition=%wide.region_10.11_spmd.clone.clone, body=%wide.region_4.10_spmd.clone.clone.sunk | while | flops 2978 | bytes 6069 | solution.py:28
  511.6 24.3 %while.129 = (s32[]{:T(128)}, f32[16,16]{1,0:T(8,128)S(1)}, f32[16,16]{1,0:T(8,128)S(1)}, f32[16,16]{1,0:T(8,128)S(1)}, s32[]{:T(128)}, /*index=5*/s32[]{:T(128)}) while((s32[]{:T(128)}, f32[16,16]{1,0:T(8,128)S(1)}, f32[16,16]{1,0:T(8,128)S(1)}, f32[16,16]{1,0:T(8,128)S(1)}, s32[]{:T(128)}, /*index=5*/s32[]{:T(128)}) %tuple.305), condition=%wide.region_17.18_spmd.clone, body=%wide.region_12.17_spmd.clone.sunk | while | flops 2626 | bytes 5984 | solution.py:43
  535.9 24.8 %while.130 = (s32[]{:T(128)}, f32[16,16]{1,0:T(8,128)S(1)}, f32[16,16]{1,0:T(8,128)S(1)}, f32[16,16]{1,0:T(8,128)S(1)}, s32[]{:T(128)}, /*index=5*/s32[]{:T(128)}, s32[]{:T(128)}) while((s32[]{:T(128)}, f32[16,16]{1,0:T(8,128)S(1)}, f32[16,16]{1,0:T(8,128)S(1)}, f32[16,16]{1,0:T(8,128)S(1)}, s32[]{:T(128)}, ...), condition=%wide.region_23.24_spmd.clone, body=%wide.region_18.23_spmd.clone.sunk | while | flops 2627 | bytes 6004 | solution.py:59
  560.9 19.6 %all_gather.15 = f32[16,8192]{1,0:T(8,128)S(1)} all-gather(f32[16,512]{1,0:T(8,128)S(1)} %convolution_subtract_fusion), channel_id=1, replica_groups=mesh['row'=16,'col'=16] {'row'}, dimensions={1}, use_global_device_ids=true | all-gather | bytes 557056 | tf_op jit(solution)/shard_map/all_gather | solution.py:132
  580.6 3.8 convolution_multiply_fusion.1
  584.5 5.2 scatter_fusion.1
  590.6 34.6 %all_gather.14 = f32[16,8192]{1,0:T(8,128)S(1)} all-gather(f32[16,512]{1,0:T(8,128)S(1)} %convolution_subtract_fusion), channel_id=1, replica_groups=mesh['row'=16,'col'=16] {'col'}, dimensions={1}, use_global_device_ids=true | all-gather | bytes 557056 | tf_op jit(solution)/shard_map/all_gather | solution.py:131
  626.0 5.2 fusion.49
  632.8 145.4 %reduce-scatter.11.cloned.1.call-done = f32[16,512]{1,0:T(8,128)} async-done(((f32[16,8192]{1,0:T(8,128)}), f32[16,512]{1,0:T(8,128)}) %reduce-scatter.11.cloned.1.call-update) | async-done | bytes 32784 | tf_op jit(solution)/shard_map/reduce_scatter | solution.py:139
  778.1 65.7 %reduce-scatter.9.cloned.1.call-done = f32[16,512]{1,0:T(8,128)} async-done(((f32[16,8192]{1,0:T(8,128)}), f32[16,512]{1,0:T(8,128)}) %reduce-scatter.9.cloned.1.call-update) | async-done | bytes 32784 | tf_op jit(solution)/shard_map/reduce_scatter | solution.py:137
  843.8 0.9 fusion.58
  844.8 79.4 %all-reduce = (f32[48,48]{0,1:T(8,128)S(1)}, f32[48,48]{1,0:T(8,128)S(1)}) all-reduce(f32[48,48]{0,1:T(8,128)S(1)} %pad_maximum_fusion.1, f32[48,48]{1,0:T(8,128)S(1)} %fusion.70), channel_id=1, replica_groups=mesh['row'=16,'col'=16] {'row','col'}, use_global_device_ids=true, to_apply=%region_35.36 | all-reduce | flops 4608 | bytes 36864 | tf_op jit(solution)/shard_map/psum | solution.py:142
  924.3 111.3 %while.136 = (s32[]{:T(128)}, f32[48,48]{1,0:T(8,128)S(1)}, f32[48,48]{1,0:T(8,128)S(1)}, s32[]{:T(128)}, s32[]{:T(128)}) while((s32[]{:T(128)}, f32[48,48]{1,0:T(8,128)S(1)}, f32[48,48]{1,0:T(8,128)S(1)}, s32[]{:T(128)}, s32[]{:T(128)}) %tuple.311), condition=%wide.region_31.32_spmd.clone.clone, body=%wide.region_25.31_spmd.clone.clone.sunk | while | flops 25826 | bytes 48693 | solution.py:28
  1035.6 79.4 %while.131 = (s32[]{:T(128)}, f32[48,48]{1,0:T(8,128)S(1)}, f32[48,48]{1,0:T(8,128)S(1)}, f32[48,48]{1,0:T(8,128)S(1)}, s32[]{:T(128)}, /*index=5*/s32[]{:T(128)}) while((s32[]{:T(128)}, f32[48,48]{1,0:T(8,128)S(1)}, f32[48,48]{1,0:T(8,128)S(1)}, f32[48,48]{1,0:T(8,128)S(1)}, s32[]{:T(128)}, /*index=5*/s32[]{:T(128)}) %tuple.314), condition=%wide.region_41.42_spmd.clone, body=%wide.region_36.41_spmd.clone.sunk | while | flops 23234 | bytes 48480 | solution.py:43
  1115.1 79.4 %while.132 = (s32[]{:T(128)}, f32[48,48]{1,0:T(8,128)S(1)}, f32[48,48]{1,0:T(8,128)S(1)}, f32[48,48]{1,0:T(8,128)S(1)}, s32[]{:T(128)}, /*index=5*/s32[]{:T(128)}) while((s32[]{:T(128)}, f32[48,48]{1,0:T(8,128)S(1)}, f32[48,48]{1,0:T(8,128)S(1)}, f32[48,48]{1,0:T(8,128)S(1)}, s32[]{:T(128)}, /*index=5*/s32[]{:T(128)}) %tuple.344), condition=%wide.region_47.48_spmd.clone, body=%wide.region_42.47_spmd.clone.sunk | while | flops 23234 | bytes 48480 | solution.py:43
  1194.8 81.8 %while.133 = (s32[]{:T(128)}, f32[48,16]{0,1:T(8,128)S(1)}, f32[48,16]{0,1:T(8,128)S(1)}, f32[48,48]{1,0:T(8,128)S(1)}, s32[]{:T(128)}, /*index=5*/s32[]{:T(128)}, s32[]{:T(128)}) while((s32[]{:T(128)}, f32[48,16]{0,1:T(8,128)S(1)}, f32[48,16]{0,1:T(8,128)S(1)}, f32[48,48]{1,0:T(8,128)S(1)}, s32[]{:T(128)}, ...), condition=%wide.region_53.54_spmd.clone, body=%wide.region_48.53_spmd.clone.sunk | while | flops 10947 | bytes 23348 | solution.py:59
  1276.8 73.6 %psum.39 = f32[16,16]{1,0:T(8,128)S(1)} all-reduce(f32[16,16]{1,0:T(8,128)S(1)} %fusion.73), channel_id=1, replica_groups=mesh['row'=16,'col'=16] {'row','col'}, use_global_device_ids=true, to_apply=%region_54.55 | all-reduce | flops 256 | bytes 2048 | tf_op jit(solution)/shard_map/psum | solution.py:152
  1350.5 37.0 %while.137 = (s32[]{:T(128)}, f32[16,16]{1,0:T(8,128)S(1)}, f32[16,16]{1,0:T(8,128)S(1)}, s32[]{:T(128)}, s32[]{:T(128)}) while((s32[]{:T(128)}, f32[16,16]{1,0:T(8,128)S(1)}, f32[16,16]{1,0:T(8,128)S(1)}, s32[]{:T(128)}, s32[]{:T(128)}) %tuple.323), condition=%wide.region_61.62_spmd.clone.clone, body=%wide.region_55.61_spmd.clone.clone.sunk | while | flops 2978 | bytes 6069 | solution.py:28
  1387.5 26.3 %while.134 = (s32[]{:T(128)}, f32[16,512]{1,0:T(8,128)S(1)}, f32[16,512]{1,0:T(8,128)S(1)}, f32[16,16]{1,0:T(8,128)S(1)}, s32[]{:T(128)}, /*index=5*/s32[]{:T(128)}) while((s32[]{:T(128)}, f32[16,512]{1,0:T(8,128)S(1)}, f32[16,512]{1,0:T(8,128)S(1)}, f32[16,16]{1,0:T(8,128)S(1)}, s32[]{:T(128)}, /*index=5*/s32[]{:T(128)}) %tuple.326), condition=%wide.region_67.68_spmd.clone, body=%wide.region_62.67_spmd.clone.sunk | while | flops 66114 | bytes 144928 | solution.py:43
  (1698 shorter events, 405.3 us)
Async XLA Ops:
  7.2 41.9 %all-gather.5.cloned.1.call-start = ((), (), s32[]{:S(2)}) async-start(), calls=%async_computation.6 | async-start | bytes 1114112 | tf_op jit(solution)/shard_map/all_gather | solution.py:114
  8.7 0.6 copy-start.4
  9.4 117.1 %all-gather.3.cloned.1.call-start = ((), (), s32[]{:S(2)}) async-start(), calls=%async_computation.4 | async-start | bytes 1114112 | tf_op jit(solution)/shard_map/all_gather | solution.py:113
  10.1 318.2 %reduce-scatter.7.cloned.1.call-start = ((), (), s32[]{:S(2)}) async-start(), calls=%async_computation.7 | async-start | bytes 1114112 | tf_op jit(solution)/shard_map/reduce_scatter | solution.py:119
  61.7 333.0 %reduce-scatter.5.cloned.1.call-start = ((), (), s32[]{:S(2)}) async-start(), calls=%async_computation.5 | async-start | bytes 1114112 | tf_op jit(solution)/shard_map/reduce_scatter | solution.py:117
  134.6 1.2 copy-start.1
  135.7 642.4 %reduce-scatter.11.cloned.1.call-start = ((), (), s32[]{:S(2)}) async-start(), calls=%async_computation.9 | async-start | bytes 557056 | tf_op jit(solution)/shard_map/reduce_scatter | solution.py:139
  560.9 715.6 %copy-start.2 = (f32[16,512]{1,0:T(8,128)}, f32[16,512]{1,0:T(8,128)S(1)}, u32[]{:S(2)}) copy-start(f32[16,512]{1,0:T(8,128)S(1)} %convolution_subtract_fusion) | copy-start | bytes 98308
  590.5 253.3 %reduce-scatter.9.cloned.1.call-start = ((), (), s32[]{:S(2)}) async-start(), calls=%async_computation.8 | async-start | bytes 557056 | tf_op jit(solution)/shard_map/reduce_scatter | solution.py:137
  626.0 6.1 copy-start.3
  1194.5 219.9 %copy-start = (f32[48,48]{1,0:T(8,128)}, f32[48,48]{1,0:T(8,128)S(1)}, u32[]{:S(2)}) copy-start(f32[48,48]{1,0:T(8,128)S(1)} %get-tuple-element.811) | copy-start | bytes 27652
Sparse Core Ops, SparseCore 0:
  9.8 39.1 all-gather.4
  51.6 74.7 all-gather.2
  130.3 198.0 reduce-scatter.6
  330.7 63.9 reduce-scatter.4
  590.6 187.4 reduce-scatter.10
  780.5 63.2 reduce-scatter.8
where the time goes:
time: 1430 us; the launch traced here: 1420 us
  waiting for transfers between devices  572 us (40%)
  other arithmetic  410 us (29%)
  blocking collectives  286 us (20%)
  loops' own time  107 us (7%)
  matrix products  21.8 us (2%)
  between operations  14.4 us (1%)
    reduce_scatter x1, waiting for transfers between devices, per_device(): lax.psum_scatter(backward, 'col', scatter_dimension=1, tiled=True)  192 us
    reduce_scatter x1, waiting for transfers between devices, per_device(): lax.psum_scatter(backward_r, 'col', scatter_dimension=1, tiled=True)  145 us
    another operation x3, loops' own time, cholesky_lower(): return lax.fori_loop(0, order_small, column_step, jnp.zeros_like(matrix))  105 us
    div x128, other arithmetic, row_step(): value = (right_row - jnp.sum(row_now[:, None] * solved, axis=0)) / pivot  87.9 us
    reduce_sum x128, other arithmetic, row_step(): pivot = jnp.sum(row_now * pick)  85.7 us
    psum x1, blocking collectives, per_device(): lax.psum((outer(basis, basis), gram_apply), ('row', 'col'))  79.4 us
    psum x1, blocking collectives, per_device(): lax.psum((outer(block_vecs, block_vecs), outer(block_vecs, image_x)), ('r...  78.8 us
    psum x1, blocking collectives, per_device(): gram_fresh = lax.psum(outer(fresh, fresh), ('row', 'col'))  73.6 us
  transfers between devices with their start and end apart: 6, of which 6 were waited for; matrix products, arithmetic and copies ran while one was open for 2% of the time, Pallas kernels for 0%

commit v1 on v0

--- a/solution.py
+++ b/solution.py
@@ -1,3 +1,4 @@
+import functools
 import math
 import jax
 import jax.numpy as jnp
@@ -5,6 +6,21 @@
 from jax.sharding import PartitionSpec as P
 
 highest = lax.Precision.HIGHEST
+
+
+def _try_all_surface(load, d_out):
+    return jnp.concatenate(
+        jax.lax.all_to_all(
+            jnp.stack([load for _ in range(jax.lax.axis_size("col"))]),
+            axis_name="col",
+            split_axis=0,
+            concat_axis=0,
+        ),
+        d_out,
+    )
+
+
+lay_points_by_axis = functools.partial(_try_all_surface, d_out=1)
 
 
 def outer(left, right):
@@ -128,7 +144,7 @@
         coefficient.T, block_vecs, precision=highest, preferred_element_type=jnp.float32
     )
     basis = jnp.concatenate([block_vecs, resid, direction], axis=0)
-    resid_cols = lax.all_gather(resid, "col", axis=1, tiled=True)
+    resid_cols = lay_points_by_axis(resid)
     resid_rows = lax.all_gather(resid, "row", axis=1, tiled=True)
     forward_r = forward_part(resid_cols, blocks, local_cols, live_mask)
     column_x = outer(basis, image_x)

time: 1430 us -> 1440 us (level)
  waiting for transfers between devices: 572 us -> 610 us
  blocking collectives: 286 us -> 251 us
    all_gather x1 -> x0, blocking collectives: 34.6 us -> none  [per_device(): resid_cols = lax.all_gather(resid, 'col', axis=1, tiled=True)]
    reduce_scatter x1, waiting for transfers between devices: 145 us -> 175 us  [per_device(): lax.psum_scatter(backward_r, 'col', scatter_dimension=1, tiled=True)]
  transfers between devices with their start and end apart: 6 -> 7, of which waited for: 6 -> 7; matrix products, arithmetic and copies ran while one was open for 2% -> 3% of each run, Pallas kernels for 0% -> 0%
where the time goes in v1:
time: 1440 us; the launch traced here: 1430 us
  waiting for transfers between devices  610 us (42%)
  other arithmetic  410 us (28%)
  blocking collectives  251 us (17%)
  loops' own time  107 us (7%)
  matrix products  21.8 us (2%)
  between operations  14.4 us (1%)
    reduce_scatter x1, waiting for transfers between devices, per_device(): lax.psum_scatter(backward, 'col', scatter_dimension=1, tiled=True)  192 us
    reduce_scatter x1, waiting for transfers between devices, per_device(): lax.psum_scatter(backward_r, 'col', scatter_dimension=1, tiled=True)  175 us
    another operation x3, loops' own time, cholesky_lower(): return lax.fori_loop(0, order_small, column_step, jnp.zeros_like(matrix))  105 us
    div x128, other arithmetic, row_step(): value = (right_row - jnp.sum(row_now[:, None] * solved, axis=0)) / pivot  87.9 us
    reduce_sum x128, other arithmetic, row_step(): pivot = jnp.sum(row_now * pick)  85.7 us
    psum x1, blocking collectives, per_device(): lax.psum((outer(basis, basis), gram_apply), ('row', 'col'))  79.4 us
    psum x1, blocking collectives, per_device(): lax.psum((outer(block_vecs, block_vecs), outer(block_vecs, image_x)), ('r...  78.8 us
    psum x1, blocking collectives, per_device(): gram_fresh = lax.psum(outer(fresh, fresh), ('row', 'col'))  73.6 us
  transfers between devices with their start and end apart: 7, of which 7 were waited for; matrix products, arithmetic and copies ran while one was open for 3% of the time, Pallas kernels for 0%

profile of v1, /device:TPU:1, one launch (start us, length us, event | category | flops | bytes accessed | tf_op | source)
XLA Modules:
  0.0 1431.8 jit_solution(15068431874640594212)
XLA Ops:
  11.9 37.2 %all-gather.5.cloned.1.call-done = f32[32,8192]{1,0:T(8,128)} async-done(((f32[32,512]{1,0:T(8,128)}), f32[32,8192]{1,0:T(8,128)}) %all-gather.5.cloned.1.call-update) | async-done | bytes 1048592 | tf_op jit(solution)/shard_map/all_gather | solution.py:130
  49.0 1.4 copy.70
  50.4 4.3 convolution_multiply_fusion
  54.9 5.7 scatter_fusion
  60.6 1.1 copy_bitcast_fusion
  62.0 64.4 %all-gather.3.cloned.1.call-done = f32[32,8192]{1,0:T(8,128)} async-done(((f32[32,512]{1,0:T(8,128)}), f32[32,8192]{1,0:T(8,128)}) %all-gather.3.cloned.1.call-update) | async-done | bytes 1048592 | tf_op jit(solution)/shard_map/all_gather | solution.py:129
  126.4 1.4 copy_bitcast_fusion.2
  128.6 6.0 fusion.45
  134.6 1.1 copy.81
  135.9 192.4 %reduce-scatter.7.cloned.1.call-done = f32[32,512]{1,0:T(8,128)} async-done(((f32[32,8192]{1,0:T(8,128)}), f32[32,512]{1,0:T(8,128)}) %reduce-scatter.7.cloned.1.call-update) | async-done | bytes 65552 | tf_op jit(solution)/shard_map/reduce_scatter | solution.py:135
  328.3 66.4 %reduce-scatter.5.cloned.1.call-done = f32[32,512]{1,0:T(8,128)} async-done(((f32[32,8192]{1,0:T(8,128)}), f32[32,512]{1,0:T(8,128)}) %reduce-scatter.5.cloned.1.call-update) | async-done | bytes 65552 | tf_op jit(solution)/shard_map/reduce_scatter | solution.py:133
  395.7 78.8 %all-reduce.1 = (f32[16,16]{0,1:T(8,128)S(1)}, f32[16,16]{1,0:T(8,128)S(1)}) all-reduce(f32[16,16]{0,1:T(8,128)S(1)} %convolution_bitcast_fusion.1, f32[16,16]{1,0:T(8,128)S(1)} %fusion.72), channel_id=1, replica_groups=mesh['row'=16,'col'=16] {'row','col'}, use_global_device_ids=true, to_apply=%region_11.12 | all-reduce | flops 512 | bytes 4096 | tf_op jit(solution)/shard_map/psum | solution.py:138
  474.5 37.0 %while.135 = (s32[]{:T(128)}, f32[16,16]{1,0:T(8,128)S(1)}, f32[16,16]{1,0:T(8,128)S(1)}, s32[]{:T(128)}, s32[]{:T(128)}) while((s32[]{:T(128)}, f32[16,16]{1,0:T(8,128)S(1)}, f32[16,16]{1,0:T(8,128)S(1)}, s32[]{:T(128)}, s32[]{:T(128)}) %tuple.304), condition=%wide.region_10.11_spmd.clone.clone, body=%wide.region_4.10_spmd.clone.clone.sunk | while | flops 2978 | bytes 6069 | solution.py:44
  511.6 24.3 %while.129 = (s32[]{:T(128)}, f32[16,16]{1,0:T(8,128)S(1)}, f32[16,16]{1,0:T(8,128)S(1)}, f32[16,16]{1,0:T(8,128)S(1)}, s32[]{:T(128)}, /*index=5*/s32[]{:T(128)}) while((s32[]{:T(128)}, f32[16,16]{1,0:T(8,128)S(1)}, f32[16,16]{1,0:T(8,128)S(1)}, f32[16,16]{1,0:T(8,128)S(1)}, s32[]{:T(128)}, /*index=5*/s32[]{:T(128)}) %tuple.307), condition=%wide.region_17.18_spmd.clone, body=%wide.region_12.17_spmd.clone.sunk | while | flops 2626 | bytes 5984 | solution.py:59
  535.9 24.8 %while.130 = (s32[]{:T(128)}, f32[16,16]{1,0:T(8,128)S(1)}, f32[16,16]{1,0:T(8,128)S(1)}, f32[16,16]{1,0:T(8,128)S(1)}, s32[]{:T(128)}, /*index=5*/s32[]{:T(128)}, s32[]{:T(128)}) while((s32[]{:T(128)}, f32[16,16]{1,0:T(8,128)S(1)}, f32[16,16]{1,0:T(8,128)S(1)}, f32[16,16]{1,0:T(8,128)S(1)}, s32[]{:T(128)}, ...), condition=%wide.region_23.24_spmd.clone, body=%wide.region_18.23_spmd.clone.sunk | while | flops 2627 | bytes 6004 | solution.py:75
  561.0 19.6 %all_gather.11 = f32[16,8192]{1,0:T(8,128)S(1)} all-gather(f32[16,512]{1,0:T(8,128)S(1)} %convolution_subtract_fusion), channel_id=1, replica_groups=mesh['row'=16,'col'=16] {'row'}, dimensions={1}, use_global_device_ids=true | all-gather | bytes 557056 | tf_op jit(solution)/shard_map/all_gather | solution.py:148
  581.4 6.1 all-to-all-start
  587.7 3.8 convolution_multiply_fusion.1
  591.6 5.2 scatter_fusion.1
  597.7 7.6 all-to-all-done
  606.7 5.2 fusion.49
  613.4 175.2 %reduce-scatter.11.cloned.1.call-done = f32[16,512]{1,0:T(8,128)} async-done(((f32[16,8192]{1,0:T(8,128)}), f32[16,512]{1,0:T(8,128)}) %reduce-scatter.11.cloned.1.call-update) | async-done | bytes 32784 | tf_op jit(solution)/shard_map/reduce_scatter | solution.py:155
  788.6 65.7 %reduce-scatter.9.cloned.1.call-done = f32[16,512]{1,0:T(8,128)} async-done(((f32[16,8192]{1,0:T(8,128)}), f32[16,512]{1,0:T(8,128)}) %reduce-scatter.9.cloned.1.call-update) | async-done | bytes 32784 | tf_op jit(solution)/shard_map/reduce_scatter | solution.py:153
  854.3 0.9 fusion.58
  855.3 79.4 %all-reduce = (f32[48,48]{0,1:T(8,128)S(1)}, f32[48,48]{1,0:T(8,128)S(1)}) all-reduce(f32[48,48]{0,1:T(8,128)S(1)} %pad_maximum_fusion.1, f32[48,48]{1,0:T(8,128)S(1)} %fusion.70), channel_id=1, replica_groups=mesh['row'=16,'col'=16] {'row','col'}, use_global_device_ids=true, to_apply=%region_35.36 | all-reduce | flops 4608 | bytes 36864 | tf_op jit(solution)/shard_map/psum | solution.py:158
  934.9 111.3 %while.136 = (s32[]{:T(128)}, f32[48,48]{1,0:T(8,128)S(1)}, f32[48,48]{1,0:T(8,128)S(1)}, s32[]{:T(128)}, s32[]{:T(128)}) while((s32[]{:T(128)}, f32[48,48]{1,0:T(8,128)S(1)}, f32[48,48]{1,0:T(8,128)S(1)}, s32[]{:T(128)}, s32[]{:T(128)}) %tuple.313), condition=%wide.region_31.32_spmd.clone.clone, body=%wide.region_25.31_spmd.clone.clone.sunk | while | flops 25826 | bytes 48693 | solution.py:44
  1046.1 79.4 %while.131 = (s32[]{:T(128)}, f32[48,48]{1,0:T(8,128)S(1)}, f32[48,48]{1,0:T(8,128)S(1)}, f32[48,48]{1,0:T(8,128)S(1)}, s32[]{:T(128)}, /*index=5*/s32[]{:T(128)}) while((s32[]{:T(128)}, f32[48,48]{1,0:T(8,128)S(1)}, f32[48,48]{1,0:T(8,128)S(1)}, f32[48,48]{1,0:T(8,128)S(1)}, s32[]{:T(128)}, /*index=5*/s32[]{:T(128)}) %tuple.316), condition=%wide.region_41.42_spmd.clone, body=%wide.region_36.41_spmd.clone.sunk | while | flops 23234 | bytes 48480 | solution.py:59
  1125.6 79.4 %while.132 = (s32[]{:T(128)}, f32[48,48]{1,0:T(8,128)S(1)}, f32[48,48]{1,0:T(8,128)S(1)}, f32[48,48]{1,0:T(8,128)S(1)}, s32[]{:T(128)}, /*index=5*/s32[]{:T(128)}) while((s32[]{:T(128)}, f32[48,48]{1,0:T(8,128)S(1)}, f32[48,48]{1,0:T(8,128)S(1)}, f32[48,48]{1,0:T(8,128)S(1)}, s32[]{:T(128)}, /*index=5*/s32[]{:T(128)}) %tuple.346), condition=%wide.region_47.48_spmd.clone, body=%wide.region_42.47_spmd.clone.sunk | while | flops 23234 | bytes 48480 | solution.py:59
  1205.3 81.8 %while.133 = (s32[]{:T(128)}, f32[48,16]{0,1:T(8,128)S(1)}, f32[48,16]{0,1:T(8,128)S(1)}, f32[48,48]{1,0:T(8,128)S(1)}, s32[]{:T(128)}, /*index=5*/s32[]{:T(128)}, s32[]{:T(128)}) while((s32[]{:T(128)}, f32[48,16]{0,1:T(8,128)S(1)}, f32[48,16]{0,1:T(8,128)S(1)}, f32[48,48]{1,0:T(8,128)S(1)}, s32[]{:T(128)}, ...), condition=%wide.region_53.54_spmd.clone, body=%wide.region_48.53_spmd.clone.sunk | while | flops 10947 | bytes 23348 | solution.py:75
  1287.4 73.6 %psum.39 = f32[16,16]{1,0:T(8,128)S(1)} all-reduce(f32[16,16]{1,0:T(8,128)S(1)} %fusion.73), channel_id=1, replica_groups=mesh['row'=16,'col'=16] {'row','col'}, use_global_device_ids=true, to_apply=%region_54.55 | all-reduce | flops 256 | bytes 2048 | tf_op jit(solution)/shard_map/psum | solution.py:168
  1361.0 37.0 %while.137 = (s32[]{:T(128)}, f32[16,16]{1,0:T(8,128)S(1)}, f32[16,16]{1,0:T(8,128)S(1)}, s32[]{:T(128)}, s32[]{:T(128)}) while((s32[]{:T(128)}, f32[16,16]{1,0:T(8,128)S(1)}, f32[16,16]{1,0:T(8,128)S(1)}, s32[]{:T(128)}, s32[]{:T(128)}) %tuple.325), condition=%wide.region_61.62_spmd.clone.clone, body=%wide.region_55.61_spmd.clone.clone.sunk | while | flops 2978 | bytes 6069 | solution.py:44
  1398.0 26.3 %while.134 = (s32[]{:T(128)}, f32[16,512]{1,0:T(8,128)S(1)}, f32[16,512]{1,0:T(8,128)S(1)}, f32[16,16]{1,0:T(8,128)S(1)}, s32[]{:T(128)}, /*index=5*/s32[]{:T(128)}) while((s32[]{:T(128)}, f32[16,512]{1,0:T(8,128)S(1)}, f32[16,512]{1,0:T(8,128)S(1)}, f32[16,16]{1,0:T(8,128)S(1)}, s32[]{:T(128)}, /*index=5*/s32[]{:T(128)}) %tuple.328), condition=%wide.region_67.68_spmd.clone, body=%wide.region_62.67_spmd.clone.sunk | while | flops 66114 | bytes 144928 | solution.py:59
  (1702 shorter events, 407.7 us)
Async XLA Ops:
  7.2 41.9 %all-gather.5.cloned.1.call-start = ((), (), s32[]{:S(2)}) async-start(), calls=%async_computation.7 | async-start | bytes 1114112 | tf_op jit(solution)/shard_map/all_gather | solution.py:130
  8.7 0.6 copy-start.4
  9.4 117.1 %all-gather.3.cloned.1.call-start = ((), (), s32[]{:S(2)}) async-start(), calls=%async_computation.5 | async-start | bytes 1114112 | tf_op jit(solution)/shard_map/all_gather | solution.py:129
  10.1 318.2 %reduce-scatter.7.cloned.1.call-start = ((), (), s32[]{:S(2)}) async-start(), calls=%async_computation.8 | async-start | bytes 1114112 | tf_op jit(solution)/shard_map/reduce_scatter | solution.py:135
  61.7 333.0 %reduce-scatter.5.cloned.1.call-start = ((), (), s32[]{:S(2)}) async-start(), calls=%async_computation.6 | async-start | bytes 1114112 | tf_op jit(solution)/shard_map/reduce_scatter | solution.py:133
  134.6 1.2 copy-start.1
  561.0 726.1 %copy-start.2 = (f32[16,512]{1,0:T(8,128)}, f32[16,512]{1,0:T(8,128)S(1)}, u32[]{:S(2)}) copy-start(f32[16,512]{1,0:T(8,128)S(1)} %convolution_subtract_fusion) | copy-start | bytes 98308
  581.4 23.8 %all-to-all-start = ((f32[16,16,512]{2,1,0:T(8,128)}), f32[16,16,512]{2,1,0:T(8,128)S(1)}, u32[]{:S(2)}, u32[]{:S(2)}) async-start(f32[16,16,512]{2,1,0:T(8,128)} %stack.2), calls=%async_computation.2 | async-start | bytes 1048576 | tf_op jit(solution)/shard_map/all_to_all | solution.py:13
  587.5 201.1 %reduce-scatter.11.cloned.1.call-start = ((), (), s32[]{:S(2)}) async-start(), calls=%async_computation.10 | async-start | bytes 557056 | tf_op jit(solution)/shard_map/reduce_scatter | solution.py:155
  597.6 256.7 %reduce-scatter.9.cloned.1.call-start = ((), (), s32[]{:S(2)}) async-start(), calls=%async_computation.9 | async-start | bytes 557056 | tf_op jit(solution)/shard_map/reduce_scatter | solution.py:153
  606.7 6.1 copy-start.3
  1205.1 219.9 %copy-start = (f32[48,48]{1,0:T(8,128)}, f32[48,48]{1,0:T(8,128)S(1)}, u32[]{:S(2)}) copy-start(f32[48,48]{1,0:T(8,128)S(1)} %get-tuple-element.811) | copy-start | bytes 27652
Sparse Core Ops, SparseCore 0:
  9.8 39.1 all-gather.4
  51.6 74.7 all-gather.2
  130.3 198.0 reduce-scatter.6
  330.7 63.9 reduce-scatter.4
  597.7 190.8 reduce-scatter.10
  791.0 63.2 reduce-scatter.8
